TPU v7x, 32 devices: a whole 2x2x4 slice. The times are simulated.
32 devices in a mesh: dp: 8 (over y, x, core), ctx: 4 (over z).
Axes of the slice: x: 2, y: 2, z: 4, core: 2. Of those that a mesh axis runs over, the one named last changes fastest.
Arguments:
- layer_input: bfloat16 [8, 2048, 1536], P('dp', 'ctx'), may hold values from -60 to 60
- attn_gain: bfloat16 [1536], P('dp'), may hold values from 0.5 to 1.5
- w_qkv: bfloat16 [1536, 3072], P('dp'), may hold values from -1 to 1
- w_out: bfloat16 [1536, 1536], P('dp'), may hold values from -2.5 to 2.5
- mlp_gain: bfloat16 [1536], P('dp'), may hold values from 0.5 to 1.5
- w_gate_up: bfloat16 [1536, 8192], P('dp'), may hold values from -0.15625 to 0.15625
- w_down: bfloat16 [4096, 1536], P('dp'), may hold values from -0.09375 to 0.09375
- cotangent: bfloat16 [8, 2048, 1536], P('dp', 'ctx'), may hold values from -6 to 6
Outputs:
- layer_output: bfloat16 [8, 2048, 1536], P('dp', 'ctx')
- input_grad: float32 [8, 2048, 1536], P('dp', 'ctx')
- attn_gain_grad: float32 [1536], P('dp')
- w_qkv_grad: float32 [1536, 3072], P('dp')
- w_out_grad: float32 [1536, 1536], P('dp')
- mlp_gain_grad: float32 [1536], P('dp')
- w_gate_up_grad: float32 [1536, 8192], P('dp')
- w_down_grad: float32 [4096, 1536], P('dp')
All inputs are finite; a program needn't handle non-finite values.
Results may differ from a plain program's by a relative error of at most 0.02.
Values may be sent and summed in bfloat16 or wider, within the bound.
No kernel may reach another device: no remote copies, remote signals or barrier semaphores. Data moves between devices by JAX's collectives and lax.ppermute only.
A program may use at most 256 MiB of HBM per device.

v0:
```python
import math
import jax
import jax.numpy as jnp
from jax import lax
from jax.sharding import PartitionSpec as P

H = 16
KVH = 8
HD = 96
FF = 4096
EPS = 1e-05
BASE = 100000.0


def rotate(values, cosines, sines):
    half = values.shape[-1] // 2
    first = values[..., :half]
    second = values[..., half:]
    return jnp.concatenate(
        [first * cosines - second * sines, second * cosines + first * sines], axis=-1
    )


def norm_back(inputs, inverse, gain, grad_normed):
    scaled = grad_normed * gain
    inner = jnp.mean(scaled * inputs, axis=-1, keepdims=True)
    grad_inputs = inverse * scaled - inputs * inverse * inverse * inverse * inner
    grad_gain = jnp.sum(grad_normed * inputs * inverse, axis=0)
    return (grad_inputs, grad_gain)


def reduce_grads(grads):
    shares = (
        lax.psum_scatter(
            grads[0].astype(jnp.bfloat16), "dp", scatter_dimension=0, tiled=True
        ).astype(jnp.float32),
        lax.psum_scatter(
            grads[1].astype(jnp.bfloat16), "dp", scatter_dimension=0, tiled=True
        ).astype(jnp.float32),
        lax.psum_scatter(
            grads[2].astype(jnp.bfloat16), "dp", scatter_dimension=0, tiled=True
        ).astype(jnp.float32),
    )
    return (
        lax.psum(shares[0].astype(jnp.bfloat16), "ctx").astype(jnp.float32),
        lax.psum(shares[1].astype(jnp.bfloat16), "ctx").astype(jnp.float32),
        lax.psum(shares[2].astype(jnp.bfloat16), "ctx").astype(jnp.float32),
    )


def visit_blocks(handler, carry, piece, length):
    rows = piece.shape[0]

    def visit(index, state):
        begin = index * length
        block = lax.dynamic_slice_in_dim(piece, index * length, length, 0)
        return handler(state, block, begin)

    return lax.fori_loop(0, rows // length, visit, carry)


def local(layer_input, attn_gain, w_qkv, w_out, mlp_gain, w_gate_up, w_down, cotangent):
    length = layer_input.shape[1]
    group = H // KVH
    q_width = H * HD
    kv_width = KVH * HD
    scale = 1.0 / math.sqrt(HD)
    seq_length = length * lax.axis_size("ctx")
    offset = lax.axis_index("ctx") * length
    q_pos = offset + jnp.arange(length, dtype=jnp.int32)
    q_last = offset + length - 1
    gain_a, whole_qkv, whole_out = (
        lax.all_gather(attn_gain, "dp", axis=0, tiled=True),
        lax.all_gather(w_qkv, "dp", axis=0, tiled=True),
        lax.all_gather(w_out, "dp", axis=0, tiled=True),
    )
    gain_a = gain_a.astype(jnp.float32)
    inputs = layer_input[0].astype(jnp.float32)
    inverse_a = lax.rsqrt(jnp.mean(inputs * inputs, axis=-1, keepdims=True) + EPS)
    normed_a = (inputs * inverse_a * gain_a).astype(jnp.bfloat16)
    proj = jnp.dot(normed_a, whole_qkv, preferred_element_type=jnp.float32)
    freq = BASE ** (-(jnp.arange(HD // 2, dtype=jnp.float32) * 2.0 / HD))
    angle = q_pos.astype(jnp.float32)[:, None] * freq[None, :]
    cosines = jnp.cos(angle)[:, None, :]
    sines = jnp.sin(angle)[:, None, :]
    q_rot = rotate(proj[:, :q_width].reshape(length, H, HD), cosines, sines).astype(jnp.bfloat16)
    k_rot = rotate(
        proj[:, q_width : q_width + kv_width].reshape(length, KVH, HD), cosines, sines
    ).astype(jnp.bfloat16)
    key_value = jnp.concatenate(
        [k_rot.reshape(length, kv_width), proj[:, q_width + kv_width :].astype(jnp.bfloat16)],
        axis=1,
    )
    query_heads = jnp.transpose(q_rot.reshape(length, KVH, group, HD), (1, 2, 0, 3))

    def block_scores(block, begin):
        count = block.shape[0]
        key_rows = block[:, :kv_width].reshape(count, KVH, HD)
        value_rows = block[:, kv_width:].reshape(count, KVH, HD)
        scores = (
            jnp.einsum("kgbd,tkd->kgbt", query_heads, key_rows, preferred_element_type=jnp.float32)
            * scale
        )
        key_pos = begin + jnp.arange(count, dtype=jnp.int32)
        visible = key_pos[None, :] <= q_pos[:, None]
        return (scores, visible, key_rows, value_rows)

    def forward_block(carry, block, begin):

        def forward_compute(state):
            scores, visible, key_rows, value_rows = block_scores(block, begin)
            scores = jnp.where(visible, scores, -1e30)
            top, total, mixed = state
            new_top = jnp.maximum(top, jnp.max(scores, axis=-1))
            fading = jnp.exp(top - new_top)
            weights = jnp.exp(scores - new_top[..., None])
            total = total * fading + jnp.sum(weights, axis=-1)
            mixed = mixed * fading[..., None] + jnp.einsum(
                "kgbt,tkd->kgbd",
                weights.astype(jnp.bfloat16),
                value_rows,
                preferred_element_type=jnp.float32,
            )
            return (new_top, total, mixed)

        return lax.cond(begin <= q_last, forward_compute, lambda state: state, carry)

    start_state = (
        jnp.full((KVH, group, length), -1e30, jnp.float32),
        jnp.zeros((KVH, group, length), jnp.float32),
        jnp.zeros((KVH, group, length, HD), jnp.float32),
    )
    top, total, mixed = visit_blocks(
        forward_block, start_state, lax.all_gather(key_value, "ctx", axis=0, tiled=True), length
    )
    attn_heads = mixed / total[..., None]
    log_total = top + jnp.log(total)
    attn_low = jnp.transpose(attn_heads, (2, 0, 1, 3)).reshape(length, q_width).astype(jnp.bfloat16)
    resid = inputs + jnp.dot(attn_low, whole_out, preferred_element_type=jnp.float32)
    gain_m, whole_gu, whole_down = (
        lax.all_gather(mlp_gain, "dp", axis=0, tiled=True),
        lax.all_gather(w_gate_up, "dp", axis=0, tiled=True),
        lax.all_gather(w_down, "dp", axis=0, tiled=True),
    )
    gain_m = gain_m.astype(jnp.float32)
    inverse_m = lax.rsqrt(jnp.mean(resid * resid, axis=-1, keepdims=True) + EPS)
    normed_m = (resid * inverse_m * gain_m).astype(jnp.bfloat16)
    gate_up = jnp.dot(normed_m, whole_gu, preferred_element_type=jnp.float32)
    gate = gate_up[:, :FF]
    upper = gate_up[:, FF:]
    sigmoid = jax.nn.sigmoid(gate)
    act = (gate * sigmoid * upper).astype(jnp.bfloat16)
    result = (resid + jnp.dot(act, whole_down, preferred_element_type=jnp.float32)).astype(
        jnp.bfloat16
    )
    grad_out = cotangent[0].astype(jnp.float32)
    grad_mlp = cotangent[0]
    down_grad = jnp.einsum("tf,td->fd", act, grad_mlp, preferred_element_type=jnp.float32)
    grad_act = jnp.einsum("td,fd->tf", grad_mlp, whole_down, preferred_element_type=jnp.float32)
    grad_gate = grad_act * upper * sigmoid * (1.0 + gate * (1.0 - sigmoid))
    grad_up = grad_act * gate * sigmoid
    grad_gu = jnp.concatenate([grad_gate, grad_up], axis=1).astype(jnp.bfloat16)
    gu_grad = jnp.einsum("td,tf->df", normed_m, grad_gu, preferred_element_type=jnp.float32)
    grad_nm = jnp.einsum("tf,df->td", grad_gu, whole_gu, preferred_element_type=jnp.float32)
    grad_res_m, gain_m_grad = norm_back(resid, inverse_m, gain_m, grad_nm)
    mlp_sums = reduce_grads((gain_m_grad, gu_grad, down_grad))
    grad_resid = grad_out + grad_res_m
    grad_branch = grad_resid.astype(jnp.bfloat16)
    out_grad = jnp.einsum("tc,td->cd", attn_low, grad_branch, preferred_element_type=jnp.float32)
    grad_attn = jnp.einsum(
        "td,cd->tc", grad_branch, whole_out, preferred_element_type=jnp.float32
    ).astype(jnp.bfloat16)
    grad_heads = jnp.transpose(grad_attn.reshape(length, KVH, group, HD), (1, 2, 0, 3))
    delta = jnp.sum(grad_heads.astype(jnp.float32) * attn_heads, axis=-1)

    def backward_block(carry, block, begin):

        def backward_compute(state):
            scores, visible, key_rows, value_rows = block_scores(block, begin)
            count = block.shape[0]
            probs = jnp.where(visible, jnp.exp(scores - log_total[..., None]), 0.0)
            grad_values = jnp.einsum(
                "kgbt,kgbd->tkd",
                probs.astype(jnp.bfloat16),
                grad_heads,
                preferred_element_type=jnp.float32,
            )
            grad_probs = jnp.einsum(
                "kgbd,tkd->kgbt", grad_heads, value_rows, preferred_element_type=jnp.float32
            )
            grad_scores = (probs * (grad_probs - delta[..., None])).astype(jnp.bfloat16)
            grad_query, grad_kv = state
            grad_query = (
                grad_query
                + jnp.einsum(
                    "kgbt,tkd->kgbd", grad_scores, key_rows, preferred_element_type=jnp.float32
                )
                * scale
            )
            grad_keys = (
                jnp.einsum(
                    "kgbt,kgbd->tkd", grad_scores, query_heads, preferred_element_type=jnp.float32
                )
                * scale
            )
            fresh = jnp.concatenate(
                [grad_keys.reshape(count, kv_width), grad_values.reshape(count, kv_width)], axis=1
            )
            current = lax.dynamic_slice_in_dim(grad_kv, begin, count, 0)
            return (grad_query, lax.dynamic_update_slice_in_dim(grad_kv, current + fresh, begin, 0))

        return lax.cond(begin <= q_last, backward_compute, lambda state: state, carry)

    back_state = (
        jnp.zeros((KVH, group, length, HD), jnp.float32),
        jnp.zeros((seq_length, 2 * kv_width), jnp.float32),
    )
    grad_query, grad_kv = visit_blocks(
        backward_block, back_state, lax.all_gather(key_value, "ctx", axis=0, tiled=True), length
    )
    own_kv = lax.psum_scatter(
        grad_kv.astype(jnp.bfloat16), "ctx", scatter_dimension=0, tiled=True
    ).astype(jnp.float32)
    grad_q = rotate(jnp.transpose(grad_query, (2, 0, 1, 3)).reshape(length, H, HD), cosines, -sines)
    grad_k = rotate(own_kv[:, :kv_width].reshape(length, KVH, HD), cosines, -sines)
    grad_proj = jnp.concatenate(
        [grad_q.reshape(length, q_width), grad_k.reshape(length, kv_width), own_kv[:, kv_width:]],
        axis=1,
    ).astype(jnp.bfloat16)
    qkv_grad = jnp.einsum("td,tc->dc", normed_a, grad_proj, preferred_element_type=jnp.float32)
    grad_na = jnp.einsum("tc,dc->td", grad_proj, whole_qkv, preferred_element_type=jnp.float32)
    grad_res_a, gain_a_grad = norm_back(inputs, inverse_a, gain_a, grad_na)
    input_grad = grad_resid + grad_res_a
    attn_sums = reduce_grads((gain_a_grad, qkv_grad, out_grad))
    return (
        result[None],
        input_grad[None],
        attn_sums[0],
        attn_sums[1],
        attn_sums[2],
        mlp_sums[0],
        mlp_sums[1],
        mlp_sums[2],
    )


def solution(mesh):
    return jax.shard_map(
        local,
        mesh=mesh,
        in_specs=(
            P("dp", "ctx", None),
            P("dp"),
            P("dp", None),
            P("dp", None),
            P("dp"),
            P("dp", None),
            P("dp", None),
            P("dp", "ctx", None),
        ),
        out_specs=(
            P("dp", "ctx", None),
            P("dp", "ctx", None),
            P("dp"),
            P("dp", None),
            P("dp", None),
            P("dp"),
            P("dp", None),
            P("dp", None),
        ),
        check_vma=False,
    )
```

profile of v0, /device:TPU:0, one launch (start us, length us, event | category | flops | bytes accessed | tf_op | source)
XLA Modules:
  0.0 1456.7 jit_solution(17770257266502485987)
XLA Ops:
  11.7 16.1 %all-reduce.5 = (bf16[1536]{0:T(1024)(128)(2,1)S(1)}, bf16[1536]{0:T(1024)(128)(2,1)S(1)}) all-reduce(bf16[1536]{0:T(1024)(128)(2,1)S(1)} %dynamic-update-slice, bf16[1536]{0:T(1024)(128)(2,1)S(1)} %dynamic-update-slice.1), channel_id=1, replica_groups=mesh['dp'=8,'ctx'=4] {'dp'}, use_global_device_ids=true, to_apply=%add | all-reduce | flops 3072 | bytes 12288
  30.7 40.7 %all-gather.6.cloned.1.call-done = bf16[1536,3072]{1,0:T(8,128)(2,1)} async-done(((bf16[192,3072]{1,0:T(8,128)(2,1)}), bf16[1536,3072]{1,0:T(8,128)(2,1)}) %all-gather.6.cloned.1.call-update) | async-done | bytes 9437200 | tf_op jit(solution)/shard_map/all_gather | solution.py:74
  95.8 104.7 %all-gather.8.cloned.1.call-done = bf16[2048,1536]{1,0:T(8,128)(2,1)} async-done(((bf16[512,1536]{1,0:T(8,128)(2,1)}), bf16[2048,1536]{1,0:T(8,128)(2,1)}) %all-gather.8.cloned.1.call-update) | async-done | bytes 6291472 | tf_op jit(solution)/shard_map/all_gather | solution.py:134
  200.5 8.7 copy.47
  209.6 30.2 %while.34 = (s32[]{:T(128)}, f32[8,2,512]{2,1,0:T(2,128)S(1)}, f32[8,2,512]{2,1,0:T(2,128)S(1)}, f32[8,2,512,96]{2,3,1,0:T(8,128)S(1)}, s32[]{:T(128)}, /*index=...) while((s32[]{:T(128)}, f32[8,2,512]{2,1,0:T(2,128)S(1)}, ...), condition=%wide.region_6.7_spmd.clone, body=%wide.region_1.6_spmd.clone.sunk | while | flops 1658602496 | bytes 64500032 | solution.py:59
  209.7 29.9 %conditional.6 = ((f32[8,2,512]{2,1,0:T(2,128)S(1)}, f32[8,2,512]{2,1,0:T(2,128)S(1)}, f32[8,2,512,96]{2,3,1,0:T(8,128)S(1)})) conditional(s32[]{:T(128)} %convert_element_type.208, (f32[8,2,512]{2,1,0:T(2,128)S(1)}, f32[8,2,512]{2,1,0:T(2,128)S(1)}, f32[8,2,512,96]{2,3,1,0:T(8,128)S(1)}) %tuple.122, (s32[]{:T(128)}, s32[]{:T(128)}, ...), branch_computations={%region_2.0_spmd, %region_3.5_spmd} | conditional | flops 1658602496 | bytes 64497760 | solution.py:126
  212.3 8.8 fusion.6
  221.1 10.0 fusion.5
  231.1 8.5 multiply_add_fusion
  249.9 116.5 %all-gather.12.cloned.1.call-done = bf16[1536,8192]{1,0:T(8,128)(2,1)} async-done(((bf16[192,8192]{1,0:T(8,128)(2,1)}), bf16[1536,8192]{1,0:T(8,128)(2,1)}) %all-gather.12.cloned.1.call-update) | async-done | bytes 25165840 | tf_op jit(solution)/shard_map/all_gather | solution.py:142
  366.4 22.4 %fusion.52 = f32[512,8192]{1,0:T(8,128)} fusion(bf16[1536,8192]{1,0:T(8,128)(2,1)} %all-gather.12.cloned.1.call-done, f32[512,1536]{1,0:T(8,128)} %get-tuple-element.693, f32[1536]{0:T(1024)S(1)} %convert_element_type.152, f32[512]{0:T(512)S(1)} %add_rsqrt_fusion), kind=kOutput, calls=%fused_computation.109 | convolution fusion | flops 12887261184 | bytes 45096960 | tf_op jit(solution)/shard_map/dot_general | solution.py:148
  388.8 51.4 %all-gather.14.cloned.1.call-done = bf16[4096,1536]{1,0:T(8,128)(2,1)} async-done(((bf16[512,1536]{1,0:T(8,128)(2,1)}), bf16[4096,1536]{1,0:T(8,128)(2,1)}) %all-gather.14.cloned.1.call-update) | async-done | bytes 12582928 | tf_op jit(solution)/shard_map/all_gather | solution.py:143
  440.2 19.2 %multiply_convert_fusion.1 = (bf16[512,4096]{1,0:T(8,128)(2,1)}, bf16[512,4096]{1,0:T(8,128)(2,1)}, bf16[512,4096]{1,0:T(8,128)(2,1)}) fusion(f32[512,8192]{1,0:T(8,128)} %fusion.52, bf16[4096,1536]{1,0:T(8,128)(2,1)} %all-gather.14.cloned.1.call-done, bf16[1,512,1536]{2,1,0:T(8,128)(2,1)} %param.23), kind=kOutput, calls=%fused_computation.39 | convolution fusion | flops 6476005376 | bytes 43515904 | tf_op jit(solution)/shard_map/td,fd->tf/dot_general | solution.py:159
  459.3 21.6 %multiply_reduce_fusion = (bf16[1536]{0:T(1024)(128)(2,1)}, f32[512]{0:T(512)S(1)}, f32[512,1536]{1,0:T(8,128)}) fusion(f32[512,1536]{1,0:T(8,128)} %get-tuple-element.693, f32[512]{0:T(512)S(1)} %add_rsqrt_fusion, f32[1536]{0:T(1024)S(1)} %convert_element_type.152, bf16[1536,8192]{1,0:T(8,128)(2,1)} %all-gather.12.cloned.1.call-done, ...), kind=kOutput, calls=%fused_computation.63 | convolution fusion | flops 12906395648 | bytes 39859200 | tf_op jit(solution)/shard_map/tf,df->td/dot_general | solution.py:164
  504.8 47.7 %while.35 = (s32[]{:T(128)}, f32[8,2,512,96]{2,3,1,0:T(8,128)S(1)}, f32[2048,1536]{0,1:T(8,128)}, s32[]{:T(128)}, bf16[2048,1536]{0,1:T(8,128)(2,1)}, /*index=5*...) while((s32[]{:T(128)}, f32[8,2,512,96]{2,3,1,0:T(8,128)S(1)}, ...), condition=%wide.region_13.14_spmd.clone, body=%wide.region_10.13_spmd.clone.sunk | while | flops 4072276992 | bytes 205631968 | solution.py:59
  505.2 47.2 %conditional.7 = ((f32[8,2,512,96]{2,3,1,0:T(8,128)S(1)}, f32[2048,1536]{0,1:T(8,128)})) conditional(s32[]{:T(128)} %convert_element_type.209, (f32[8,2,512,96]{2,3,1,0:T(8,128)S(1)}, f32[2048,1536]{0,1:T(8,128)}) %tuple.125, (s32[]{:T(128)}, s32[]{:T(128)}, bf16[2048,1536]{0,1:T(8,128)(2,1)}, bf16[8,2,512,96]{2,3,1,0:T(8,128)(2,1)}, ...), branch_computations={%region_11.11_spmd, %region_12.12_spmd} | conditional | flops 4072276992 | bytes 205629664 | solution.py:212
  512.8 10.5 fusion.14
  530.6 10.7 fusion.16
  552.5 8.3 convert_element_type.160
  568.2 11.6 convolution_convert_fusion.1
  581.4 231.7 %reduce-scatter.6.cloned.1.call-done = bf16[512,1536]{0,1:T(8,128)(2,1)} async-done(((bf16[2048,1536]{0,1:T(8,128)(2,1)}), bf16[512,1536]{0,1:T(8,128)(2,1)}) %reduce-scatter.6.cloned.1.call-update) | async-done | bytes 1572880 | tf_op jit(solution)/shard_map/reduce_scatter | solution.py:221
  816.6 9.8 convolution_convert_fusion.2
  828.7 21.2 %convolution_convert_fusion = bf16[1536,8192]{1,0:T(8,128)(2,1)} fusion(bf16[512,4096]{1,0:T(8,128)(2,1)} %get-tuple-element.675, bf16[512,4096]{1,0:T(8,128)(2,1)} %get-tuple-element.674, f32[512,1536]{1,0:T(8,128)S(1)} %copy-done.11, f32[1536]{0:T(1024)S(1)} %copy-done.26, f32[512]{0:T(512)S(1)} %copy-done.30), kind=kOutput, calls=%fused_computation.34 | convolution fusion | flops 12916621312 | bytes 36708352 | tf_op jit(solution)/shard_map/td,tf->df/dot_general | solution.py:163
  850.2 20.7 %reduce-scatter.10.cloned.1.call-done = bf16[192,1536]{1,0:T(8,128)(2,1)} async-done(((bf16[1536,1536]{1,0:T(8,128)(2,1)}), bf16[192,1536]{1,0:T(8,128)(2,1)}) %reduce-scatter.10.cloned.1.call-update) | async-done | bytes 589840 | tf_op jit(solution)/shard_map/reduce_scatter | solution.py:40
  871.0 95.8 %reduce-scatter.14.cloned.1.call-done = bf16[512,1536]{1,0:T(8,128)(2,1)} async-done(((bf16[4096,1536]{1,0:T(8,128)(2,1)}), bf16[512,1536]{1,0:T(8,128)(2,1)}) %reduce-scatter.14.cloned.1.call-update) | async-done | bytes 1572880 | tf_op jit(solution)/shard_map/reduce_scatter | solution.py:40
  966.8 80.4 %reduce-scatter.8.cloned.1.call-done = bf16[192,3072]{1,0:T(8,128)(2,1)} async-done(((bf16[1536,3072]{1,0:T(8,128)(2,1)}), bf16[192,3072]{1,0:T(8,128)(2,1)}) %reduce-scatter.8.cloned.1.call-update) | async-done | bytes 1179664 | tf_op jit(solution)/shard_map/reduce_scatter | solution.py:37
  1047.1 159.8 %reduce-scatter.12.cloned.1.call-done = bf16[192,8192]{1,0:T(8,128)(2,1)} async-done(((bf16[1536,8192]{1,0:T(8,128)(2,1)}), bf16[192,8192]{1,0:T(8,128)(2,1)}) %reduce-scatter.12.cloned.1.call-update) | async-done | bytes 3145744 | tf_op jit(solution)/shard_map/reduce_scatter | solution.py:37
  1207.7 11.9 fusion.36
  1219.6 11.0 fusion.34
  1230.6 13.6 all-reduce.4
  1244.4 12.3 all-reduce.6
  1262.8 176.3 %all-reduce.10.cloned.1.call-done = (bf16[192,3072]{1,0:T(8,128)(2,1)}, bf16[192,1536]{1,0:T(8,128)(2,1)}, bf16[192,8192]{1,0:T(8,128)(2,1)}, bf16[512,1536]{1,0:T(8,128)(2,1)}) async-done(((bf16[192,3072]{1,0:T(8,128)(2,1)}, bf16[192,1536]{1,0:T(8,128)(2,1)}, bf16[192,8192]{1,0:T(8,128)(2,1)}, bf16[512,1536]{1,0:T(8,128)(2,1)}), (bf16[192,3072]{1,0:T(8,128)(2,1)}, bf16[192,1536]{1,0:T(8,128)(2,1)}, ...) | async-done | bytes 6488080 | tf_op jit(solution)/shard_map/psum | solution.py:46
  (169 shorter events, 126.0 us)
Async XLA Ops:
  7.2 64.2 %copy-start.6 = (bf16[1,512,1536]{2,1,0:T(8,128)(2,1)S(1)}, bf16[1,512,1536]{2,1,0:T(8,128)(2,1)}, u32[]{:S(2)}) copy-start(bf16[1,512,1536]{2,1,0:T(8,128)(2,1)} %param.16) | copy-start | bytes 4718596
  7.2 64.2 %all-gather.6.cloned.1.call-start = ((), (), s32[]{:S(2)}) async-start(), calls=%async_computation.5 | async-start | bytes 10616832 | tf_op jit(solution)/shard_map/all_gather | solution.py:74
  7.9 192.6 %all-gather.8.cloned.1.call-start = ((), (), s32[]{:S(2)}) async-start(), calls=%async_computation.6 | async-start | bytes 7864320 | tf_op jit(solution)/shard_map/all_gather | solution.py:134
  27.8 51.3 %copy-start.23 = (f32[1536]{0:T(1024)}, f32[1536]{0:T(1024)S(1)}, u32[]{:S(2)}) copy-start(f32[1536]{0:T(1024)S(1)} %convert_element_type.145) | copy-start | bytes 18436
  29.6 49.5 %copy-start.27 = (f32[512]{0:T(512)}, f32[512]{0:T(512)S(1)}, u32[]{:S(2)}) copy-start(f32[512]{0:T(512)S(1)} %add_rsqrt_fusion.1) | copy-start | bytes 6148
  30.7 63.3 %copy-start.13 = (f32[512,48]{0,1:T(8,128)}, f32[512,48]{0,1:T(8,128)S(1)}, u32[]{:S(2)}) copy-start(f32[512,48]{0,1:T(8,128)S(1)} %get-tuple-element.689) | copy-start | bytes 294916
  79.1 2.9 copy-start.9
  85.1 156.3 %all-gather.10.cloned.1.call-start = ((), (), s32[]{:S(2)}) async-start(), calls=%async_computation.7 | async-start | bytes 5308416 | tf_op jit(solution)/shard_map/all_gather | solution.py:75
  85.8 280.6 %all-gather.12.cloned.1.call-start = ((), (), s32[]{:S(2)}) async-start(), calls=%async_computation.8 | async-start | bytes 28311552 | tf_op jit(solution)/shard_map/all_gather | solution.py:142
  86.4 353.8 %all-gather.14.cloned.1.call-start = ((), (), s32[]{:S(2)}) async-start(), calls=%async_computation.9 | async-start | bytes 14155776 | tf_op jit(solution)/shard_map/all_gather | solution.py:143
  87.0 726.2 %reduce-scatter.6.cloned.1.call-start = ((), (), s32[]{:S(2)}) async-start(), calls=%async_computation.10 | async-start | bytes 7864320 | tf_op jit(solution)/shard_map/reduce_scatter | solution.py:221
  87.0 393.9 %copy-start.25 = (f32[1536]{0:T(1024)}, f32[1536]{0:T(1024)S(1)}, u32[]{:S(2)}) copy-start(f32[1536]{0:T(1024)S(1)} %convert_element_type.152) | copy-start | bytes 18436
  249.3 231.7 %copy-start.29 = (f32[512]{0:T(512)}, f32[512]{0:T(512)S(1)}, u32[]{:S(2)}) copy-start(f32[512]{0:T(512)S(1)} %add_rsqrt_fusion) | copy-start | bytes 6148
  505.2 3.5 copy-start.1
  512.5 10.7 copy-start
  541.3 6.6 copy-start.3
  547.9 4.5 copy-start.2
  560.8 310.2 %reduce-scatter.10.cloned.1.call-start = ((), (), s32[]{:S(2)}) async-start(), calls=%async_computation.12 | async-start | bytes 5308416 | tf_op jit(solution)/shard_map/reduce_scatter | solution.py:40
  568.1 398.7 %reduce-scatter.14.cloned.1.call-start = ((), (), s32[]{:S(2)}) async-start(), calls=%async_computation.14 | async-start | bytes 14155776 | tf_op jit(solution)/shard_map/reduce_scatter | solution.py:40
  579.8 467.3 %reduce-scatter.8.cloned.1.call-start = ((), (), s32[]{:S(2)}) async-start(), calls=%async_computation.11 | async-start | bytes 10616832 | tf_op jit(solution)/shard_map/reduce_scatter | solution.py:37
  581.4 233.8 %copy-start.15 = (bf16[512,16,96]{0,2,1:T(8,128)(2,1)}, bf16[512,16,96]{0,2,1:T(8,128)(2,1)S(1)}, u32[]{:S(2)}) copy-start(bf16[512,16,96]{0,2,1:T(8,128)(2,1)S(1)} %pad_maximum_fusion.5) | copy-start | bytes 4718596
  826.5 2.2 copy-start.30
  826.5 380.5 %reduce-scatter.12.cloned.1.call-start = ((), (), s32[]{:S(2)}) async-start(), calls=%async_computation.13 | async-start | bytes 28311552 | tf_op jit(solution)/shard_map/reduce_scatter | solution.py:37
  850.0 589.1 %all-reduce.10.cloned.1.call-start = ((), (), s32[]{:S(2)}) async-start(), calls=%async_computation.15 | async-start | bytes 12976128 | tf_op jit(solution)/shard_map/psum | solution.py:46
  1207.6 11.9 copy-start.8
  1207.6 11.9 copy-start.16
  1207.6 11.9 copy-start.20
  1207.7 11.9 copy-start.22
  1219.6 11.0 copy-start.31
  1219.6 38.2 %copy-start.5 = (f32[512,1536]{1,0:T(8,128)S(1)}, f32[512,1536]{1,0:T(8,128)}, u32[]{:S(2)}) copy-start(f32[512,1536]{1,0:T(8,128)} %copy-done.4) | copy-start | bytes 9437188
  1439.1 5.3 copy-start.12
  1444.4 3.4 copy-start.17
  (11 other events, 16.8 us)
Sparse Core Ops, SparseCore 0:
  9.9 61.4 all-gather.5
  85.2 115.3 all-gather.7
  202.4 36.9 all-gather.9
  241.2 125.1 all-gather.11
  368.1 71.9 all-gather.13
  560.9 252.2 reduce-scatter.5
  816.6 54.2 reduce-scatter.9
  874.5 92.2 reduce-scatter.13
  970.3 76.8 reduce-scatter.7
  1050.6 156.3 reduce-scatter.11
  1209.6 229.4 all-reduce.9
where the time goes:
time: 1460 us
  waiting for transfers between devices  1080 us (74%)
  matrix products  214 us (15%)
  other arithmetic  56.8 us (4%)
  local copies, waits for them, and re-layouts  46.2 us (3%)
  blocking collectives  42 us (3%)
  between operations  15.8 us (1%)
    reduce_scatter x2, waiting for transfers between devices, reduce_grads(): lax.psum_scatter(grads[1].astype(jnp.bfloat16), 'dp', scatter_dimension=0...  240 us
    reduce_scatter x1, waiting for transfers between devices, local(): lax.psum_scatter(grad_kv.astype(jnp.bfloat16), 'ctx', scatter_dimension=0...  232 us
    psum x1, waiting for transfers between devices, reduce_grads(): lax.psum(shares[1].astype(jnp.bfloat16), 'ctx').astype(jnp.float32)  176 us
    reduce_scatter x2, waiting for transfers between devices, reduce_grads(): lax.psum_scatter(grads[2].astype(jnp.bfloat16), 'dp', scatter_dimension=0...  117 us
    all_gather x1, waiting for transfers between devices, local(): lax.all_gather(w_gate_up, 'dp', axis=0, tiled=True)  116 us
    all_gather x1, waiting for transfers between devices, local(): lax.all_gather(key_value, 'ctx', axis=0, tiled=True)  105 us
    all_gather x1, waiting for transfers between devices, local(): lax.all_gather(w_down, 'dp', axis=0, tiled=True)  51.4 us
    all_gather x1, waiting for transfers between devices, local(): lax.all_gather(w_qkv, 'dp', axis=0, tiled=True)  40.7 us
  transfers between devices with their start and end apart: 11, of which 10 were waited for; matrix products, arithmetic and copies ran while one was open for 12% of the time, Pallas kernels for 0%

commit v1 on v0

--- a/solution.py
+++ b/solution.py
@@ -43,7 +43,7 @@
     )
     return (
         lax.psum(shares[0].astype(jnp.bfloat16), "ctx").astype(jnp.float32),
-        lax.psum(shares[1].astype(jnp.bfloat16), "ctx").astype(jnp.float32),
+        jnp.sum(lax.all_gather(shares[1].astype(jnp.bfloat16), "ctx"), axis=0).astype(jnp.float32),
         lax.psum(shares[2].astype(jnp.bfloat16), "ctx").astype(jnp.float32),
     )
 

time: 1460 us -> 1630 us (1.12)
  waiting for transfers between devices: 1080 us -> 1240 us
    all_gather x0 -> x2, waiting for transfers between devices: none -> 297 us  [reduce_grads(): lax.all_gather(shares[1].astype(jnp.bfloat16), 'ctx')]
    psum x1, waiting for transfers between devices: 176 us -> 35.4 us  [reduce_grads(): lax.psum(shares[2].astype(jnp.bfloat16), 'ctx').astype(jnp.float32)]
  transfers between devices with their start and end apart: 11 -> 13, of which waited for: 10 -> 12; matrix products, arithmetic and copies ran while one was open for 12% -> 11% of each run, Pallas kernels for 0% -> 0%
where the time goes in v1:
time: 1630 us; the launch traced here: 1620 us
  waiting for transfers between devices  1240 us (76%)
  matrix products  214 us (13%)
  other arithmetic  67.4 us (4%)
  local copies, waits for them, and re-layouts  45.8 us (3%)
  blocking collectives  41.5 us (3%)
    all_gather x2, waiting for transfers between devices, reduce_grads(): lax.all_gather(shares[1].astype(jnp.bfloat16), 'ctx')  297 us
    reduce_scatter x2, waiting for transfers between devices, reduce_grads(): lax.psum_scatter(grads[1].astype(jnp.bfloat16), 'dp', scatter_dimension=0...  240 us
    reduce_scatter x1, waiting for transfers between devices, local(): lax.psum_scatter(grad_kv.astype(jnp.bfloat16), 'ctx', scatter_dimension=0...  231 us
    reduce_scatter x2, waiting for transfers between devices, reduce_grads(): lax.psum_scatter(grads[2].astype(jnp.bfloat16), 'dp', scatter_dimension=0...  117 us
    all_gather x1, waiting for transfers between devices, local(): lax.all_gather(w_gate_up, 'dp', axis=0, tiled=True)  116 us
    all_gather x1, waiting for transfers between devices, local(): lax.all_gather(key_value, 'ctx', axis=0, tiled=True)  105 us
    all_gather x1, waiting for transfers between devices, local(): lax.all_gather(w_down, 'dp', axis=0, tiled=True)  51.1 us
    all_gather x1, waiting for transfers between devices, local(): lax.all_gather(w_qkv, 'dp', axis=0, tiled=True)  40.7 us
  transfers between devices with their start and end apart: 13, of which 12 were waited for; matrix products, arithmetic and copies ran while one was open for 11% of the time, Pallas kernels for 0%

profile of v1, /device:TPU:0, one launch (start us, length us, event | category | flops | bytes accessed | tf_op | source)
XLA Modules:
  0.0 1623.2 jit_solution(2531388877390008011)
XLA Ops:
  11.7 16.1 all-reduce.5
  30.7 40.7 %all-gather.10.cloned.1.call-done = bf16[1536,3072]{1,0:T(8,128)(2,1)} async-done(((bf16[192,3072]{1,0:T(8,128)(2,1)}), bf16[1536,3072]{1,0:T(8,128)(2,1)}) %all-gather.10.cloned.1.call-update) | async-done | bytes 9437200 | tf_op jit(solution)/shard_map/all_gather | solution.py:74
  95.6 105.0 %all-gather.12.cloned.1.call-done = bf16[2048,1536]{1,0:T(8,128)(2,1)} async-done(((bf16[512,1536]{1,0:T(8,128)(2,1)}), bf16[2048,1536]{1,0:T(8,128)(2,1)}) %all-gather.12.cloned.1.call-update) | async-done | bytes 6291472 | tf_op jit(solution)/shard_map/all_gather | solution.py:134
  200.6 8.7 copy.47
  209.7 30.2 %while.34 = (s32[]{:T(128)}, f32[8,2,512]{2,1,0:T(2,128)S(1)}, f32[8,2,512]{2,1,0:T(2,128)S(1)}, f32[8,2,512,96]{2,3,1,0:T(8,128)S(1)}, s32[]{:T(128)}, /*index=...) while((s32[]{:T(128)}, f32[8,2,512]{2,1,0:T(2,128)S(1)}, ...), condition=%wide.region_6.7_spmd.clone, body=%wide.region_1.6_spmd.clone.sunk | while | flops 1658602496 | bytes 64500032 | solution.py:59
  209.7 29.9 %conditional.6 = ((f32[8,2,512]{2,1,0:T(2,128)S(1)}, f32[8,2,512]{2,1,0:T(2,128)S(1)}, f32[8,2,512,96]{2,3,1,0:T(8,128)S(1)})) conditional(s32[]{:T(128)} %convert_element_type.212, (f32[8,2,512]{2,1,0:T(2,128)S(1)}, f32[8,2,512]{2,1,0:T(2,128)S(1)}, f32[8,2,512,96]{2,3,1,0:T(8,128)S(1)}) %tuple.122, (s32[]{:T(128)}, s32[]{:T(128)}, ...), branch_computations={%region_2.0_spmd, %region_3.5_spmd} | conditional | flops 1658602496 | bytes 64497760 | solution.py:126
  212.3 8.8 fusion.6
  221.1 10.0 fusion.5
  250.0 116.5 %all-gather.16.cloned.1.call-done = bf16[1536,8192]{1,0:T(8,128)(2,1)} async-done(((bf16[192,8192]{1,0:T(8,128)(2,1)}), bf16[1536,8192]{1,0:T(8,128)(2,1)}) %all-gather.16.cloned.1.call-update) | async-done | bytes 25165840 | tf_op jit(solution)/shard_map/all_gather | solution.py:142
  366.4 22.6 %fusion.52 = f32[512,8192]{1,0:T(8,128)} fusion(bf16[1536,8192]{1,0:T(8,128)(2,1)} %all-gather.16.cloned.1.call-done, f32[512,1536]{1,0:T(8,128)} %get-tuple-element.691, f32[1536]{0:T(1024)S(1)} %convert_element_type.156, f32[512]{0:T(512)S(1)} %add_rsqrt_fusion), kind=kOutput, calls=%fused_computation.109 | convolution fusion | flops 12887261184 | bytes 45096960 | tf_op jit(solution)/shard_map/dot_general | solution.py:148
  389.1 51.1 %all-gather.18.cloned.1.call-done = bf16[4096,1536]{1,0:T(8,128)(2,1)} async-done(((bf16[512,1536]{1,0:T(8,128)(2,1)}), bf16[4096,1536]{1,0:T(8,128)(2,1)}) %all-gather.18.cloned.1.call-update) | async-done | bytes 12582928 | tf_op jit(solution)/shard_map/all_gather | solution.py:143
  440.2 19.2 %multiply_convert_fusion.1 = (bf16[512,4096]{1,0:T(8,128)(2,1)}, bf16[512,4096]{1,0:T(8,128)(2,1)}, bf16[512,4096]{1,0:T(8,128)(2,1)}) fusion(f32[512,8192]{1,0:T(8,128)} %fusion.52, bf16[4096,1536]{1,0:T(8,128)(2,1)} %all-gather.18.cloned.1.call-done, bf16[1,512,1536]{2,1,0:T(8,128)(2,1)} %param.23), kind=kOutput, calls=%fused_computation.39 | convolution fusion | flops 6476005376 | bytes 43515904 | tf_op jit(solution)/shard_map/td,fd->tf/dot_general | solution.py:159
  459.4 21.6 %multiply_reduce_fusion = (bf16[1536]{0:T(1024)(128)(2,1)}, f32[512]{0:T(512)S(1)}, f32[512,1536]{1,0:T(8,128)}) fusion(f32[512,1536]{1,0:T(8,128)} %get-tuple-element.691, f32[512]{0:T(512)S(1)} %add_rsqrt_fusion, f32[1536]{0:T(1024)S(1)} %convert_element_type.156, bf16[1536,8192]{1,0:T(8,128)(2,1)} %all-gather.16.cloned.1.call-done, ...), kind=kOutput, calls=%fused_computation.63 | convolution fusion | flops 12906395648 | bytes 39859200 | tf_op jit(solution)/shard_map/tf,df->td/dot_general | solution.py:164
  504.8 47.4 %while.35 = (s32[]{:T(128)}, f32[8,2,512,96]{2,3,1,0:T(8,128)S(1)}, f32[2048,1536]{0,1:T(8,128)}, s32[]{:T(128)}, bf16[2048,1536]{0,1:T(8,128)(2,1)}, /*index=5*...) while((s32[]{:T(128)}, f32[8,2,512,96]{2,3,1,0:T(8,128)S(1)}, ...), condition=%wide.region_13.14_spmd.clone, body=%wide.region_10.13_spmd.clone.sunk | while | flops 4072276992 | bytes 205631968 | solution.py:59
  505.0 47.2 %conditional.7 = ((f32[8,2,512,96]{2,3,1,0:T(8,128)S(1)}, f32[2048,1536]{0,1:T(8,128)})) conditional(s32[]{:T(128)} %convert_element_type.213, (f32[8,2,512,96]{2,3,1,0:T(8,128)S(1)}, f32[2048,1536]{0,1:T(8,128)}) %tuple.125, (s32[]{:T(128)}, s32[]{:T(128)}, bf16[2048,1536]{0,1:T(8,128)(2,1)}, bf16[8,2,512,96]{2,3,1,0:T(8,128)(2,1)}, ...), branch_computations={%region_11.11_spmd, %region_12.12_spmd} | conditional | flops 4072276992 | bytes 205629664 | solution.py:212
  512.6 10.5 fusion.14
  530.4 10.7 fusion.16
  568.2 11.6 convolution_convert_fusion.1
  581.5 231.5 %reduce-scatter.6.cloned.1.call-done = bf16[512,1536]{0,1:T(8,128)(2,1)} async-done(((bf16[2048,1536]{0,1:T(8,128)(2,1)}), bf16[512,1536]{0,1:T(8,128)(2,1)}) %reduce-scatter.6.cloned.1.call-update) | async-done | bytes 1572880 | tf_op jit(solution)/shard_map/reduce_scatter | solution.py:221
  816.4 9.9 convolution_convert_fusion.2
  828.6 21.2 %convolution_convert_fusion = bf16[1536,8192]{1,0:T(8,128)(2,1)} fusion(bf16[512,4096]{1,0:T(8,128)(2,1)} %get-tuple-element.673, bf16[512,4096]{1,0:T(8,128)(2,1)} %get-tuple-element.672, f32[512,1536]{1,0:T(8,128)S(1)} %copy-done.11, f32[1536]{0:T(1024)S(1)} %copy-done.24, f32[512]{0:T(512)S(1)} %copy-done.28), kind=kOutput, calls=%fused_computation.34 | convolution fusion | flops 12916621312 | bytes 36708352 | tf_op jit(solution)/shard_map/td,tf->df/dot_general | solution.py:163
  849.9 20.8 %reduce-scatter.10.cloned.1.call-done = bf16[192,1536]{1,0:T(8,128)(2,1)} async-done(((bf16[1536,1536]{1,0:T(8,128)(2,1)}), bf16[192,1536]{1,0:T(8,128)(2,1)}) %reduce-scatter.10.cloned.1.call-update) | async-done | bytes 589840 | tf_op jit(solution)/shard_map/reduce_scatter | solution.py:40
  870.7 95.8 %reduce-scatter.14.cloned.1.call-done = bf16[512,1536]{1,0:T(8,128)(2,1)} async-done(((bf16[4096,1536]{1,0:T(8,128)(2,1)}), bf16[512,1536]{1,0:T(8,128)(2,1)}) %reduce-scatter.14.cloned.1.call-update) | async-done | bytes 1572880 | tf_op jit(solution)/shard_map/reduce_scatter | solution.py:40
  966.6 80.3 %reduce-scatter.8.cloned.1.call-done = bf16[192,3072]{1,0:T(8,128)(2,1)} async-done(((bf16[1536,3072]{1,0:T(8,128)(2,1)}), bf16[192,3072]{1,0:T(8,128)(2,1)}) %reduce-scatter.8.cloned.1.call-update) | async-done | bytes 1179664 | tf_op jit(solution)/shard_map/reduce_scatter | solution.py:37
  1047.0 159.8 %reduce-scatter.12.cloned.1.call-done = bf16[192,8192]{1,0:T(8,128)(2,1)} async-done(((bf16[1536,8192]{1,0:T(8,128)(2,1)}), bf16[192,8192]{1,0:T(8,128)(2,1)}) %reduce-scatter.12.cloned.1.call-update) | async-done | bytes 3145744 | tf_op jit(solution)/shard_map/reduce_scatter | solution.py:37
  1207.4 11.9 fusion.36
  1219.3 11.1 fusion.34
  1230.4 13.5 all-reduce.4
  1244.1 11.9 all-reduce.6
  1262.3 35.4 %all-reduce.10.cloned.1.call-done = (bf16[192,1536]{1,0:T(8,128)(2,1)}, bf16[512,1536]{1,0:T(8,128)(2,1)}) async-done(((bf16[192,1536]{1,0:T(8,128)(2,1)}, bf16[512,1536]{1,0:T(8,128)(2,1)}), (bf16[192,1536]{1,0:T(8,128)(2,1)}, bf16[512,1536]{1,0:T(8,128)(2,1)})) %all-reduce.10.cloned.1.call-update) | async-done | bytes 2162704 | tf_op jit(solution)/shard_map/psum | solution.py:47
  1303.4 84.2 %all-gather.20.cloned.1.call-done = bf16[768,3072]{1,0:T(8,128)(2,1)} async-done(((bf16[192,3072]{1,0:T(8,128)(2,1)}), bf16[768,3072]{1,0:T(8,128)(2,1)}) %all-gather.20.cloned.1.call-update) | async-done | bytes 4718608 | tf_op jit(solution)/shard_map/all_gather | solution.py:46
  1392.5 213.2 %all-gather.22.cloned.1.call-done = bf16[768,8192]{1,0:T(8,128)(2,1)} async-done(((bf16[192,8192]{1,0:T(8,128)(2,1)}), bf16[768,8192]{1,0:T(8,128)(2,1)}) %all-gather.22.cloned.1.call-update) | async-done | bytes 12582928 | tf_op jit(solution)/shard_map/all_gather | solution.py:46
  (173 shorter events, 153.3 us)
Async XLA Ops:
  7.2 64.2 %copy-start.6 = (bf16[1,512,1536]{2,1,0:T(8,128)(2,1)S(1)}, bf16[1,512,1536]{2,1,0:T(8,128)(2,1)}, u32[]{:S(2)}) copy-start(bf16[1,512,1536]{2,1,0:T(8,128)(2,1)} %param.16) | copy-start | bytes 4718596
  7.2 64.2 %all-gather.10.cloned.1.call-start = ((), (), s32[]{:S(2)}) async-start(), calls=%async_computation.5 | async-start | bytes 10616832 | tf_op jit(solution)/shard_map/all_gather | solution.py:74
  7.9 192.7 %all-gather.12.cloned.1.call-start = ((), (), s32[]{:S(2)}) async-start(), calls=%async_computation.6 | async-start | bytes 7864320 | tf_op jit(solution)/shard_map/all_gather | solution.py:134
  27.8 51.4 %copy-start.21 = (f32[1536]{0:T(1024)}, f32[1536]{0:T(1024)S(1)}, u32[]{:S(2)}) copy-start(f32[1536]{0:T(1024)S(1)} %convert_element_type.149) | copy-start | bytes 18436
  29.6 49.5 %copy-start.25 = (f32[512]{0:T(512)}, f32[512]{0:T(512)S(1)}, u32[]{:S(2)}) copy-start(f32[512]{0:T(512)S(1)} %add_rsqrt_fusion.1) | copy-start | bytes 6148
  30.7 63.0 %copy-start.12 = (f32[512,48]{0,1:T(8,128)}, f32[512,48]{0,1:T(8,128)S(1)}, u32[]{:S(2)}) copy-start(f32[512,48]{0,1:T(8,128)S(1)} %get-tuple-element.687) | copy-start | bytes 294916
  79.2 2.9 copy-start.9
  85.1 156.3 %all-gather.14.cloned.1.call-start = ((), (), s32[]{:S(2)}) async-start(), calls=%async_computation.7 | async-start | bytes 5308416 | tf_op jit(solution)/shard_map/all_gather | solution.py:75
  85.8 280.6 %all-gather.16.cloned.1.call-start = ((), (), s32[]{:S(2)}) async-start(), calls=%async_computation.8 | async-start | bytes 28311552 | tf_op jit(solution)/shard_map/all_gather | solution.py:142
  86.4 353.8 %all-gather.18.cloned.1.call-start = ((), (), s32[]{:S(2)}) async-start(), calls=%async_computation.9 | async-start | bytes 14155776 | tf_op jit(solution)/shard_map/all_gather | solution.py:143
  87.0 726.0 %reduce-scatter.6.cloned.1.call-start = ((), (), s32[]{:S(2)}) async-start(), calls=%async_computation.10 | async-start | bytes 7864320 | tf_op jit(solution)/shard_map/reduce_scatter | solution.py:221
  87.1 394.0 %copy-start.23 = (f32[1536]{0:T(1024)}, f32[1536]{0:T(1024)S(1)}, u32[]{:S(2)}) copy-start(f32[1536]{0:T(1024)S(1)} %convert_element_type.156) | copy-start | bytes 18436
  249.4 231.7 %copy-start.27 = (f32[512]{0:T(512)}, f32[512]{0:T(512)S(1)}, u32[]{:S(2)}) copy-start(f32[512]{0:T(512)S(1)} %add_rsqrt_fusion) | copy-start | bytes 6148
  505.0 3.5 copy-start.1
  512.3 10.7 copy-start
  541.1 6.6 copy-start.3
  547.7 4.5 copy-start.2
  560.6 310.2 %reduce-scatter.10.cloned.1.call-start = ((), (), s32[]{:S(2)}) async-start(), calls=%async_computation.12 | async-start | bytes 5308416 | tf_op jit(solution)/shard_map/reduce_scatter | solution.py:40
  568.2 398.4 %reduce-scatter.14.cloned.1.call-start = ((), (), s32[]{:S(2)}) async-start(), calls=%async_computation.14 | async-start | bytes 14155776 | tf_op jit(solution)/shard_map/reduce_scatter | solution.py:40
  579.9 467.0 %reduce-scatter.8.cloned.1.call-start = ((), (), s32[]{:S(2)}) async-start(), calls=%async_computation.11 | async-start | bytes 10616832 | tf_op jit(solution)/shard_map/reduce_scatter | solution.py:37
  581.5 233.6 %copy-start.14 = (bf16[512,16,96]{0,2,1:T(8,128)(2,1)}, bf16[512,16,96]{0,2,1:T(8,128)(2,1)S(1)}, u32[]{:S(2)}) copy-start(bf16[512,16,96]{0,2,1:T(8,128)(2,1)S(1)} %pad_maximum_fusion.5) | copy-start | bytes 4718596
  826.4 2.3 copy-start.28
  826.4 380.3 %reduce-scatter.12.cloned.1.call-start = ((), (), s32[]{:S(2)}) async-start(), calls=%async_computation.13 | async-start | bytes 28311552 | tf_op jit(solution)/shard_map/reduce_scatter | solution.py:37
  849.9 447.8 %all-reduce.10.cloned.1.call-start = ((), (), s32[]{:S(2)}) async-start(), calls=%async_computation.17 | async-start | bytes 4325376 | tf_op jit(solution)/shard_map/psum | solution.py:47
  966.6 421.0 %all-gather.20.cloned.1.call-start = ((), (), s32[]{:S(2)}) async-start(), calls=%async_computation.15 | async-start | bytes 5898240 | tf_op jit(solution)/shard_map/all_gather | solution.py:46
  1046.9 558.8 %all-gather.22.cloned.1.call-start = ((), (), s32[]{:S(2)}) async-start(), calls=%async_computation.16 | async-start | bytes 15728640 | tf_op jit(solution)/shard_map/all_gather | solution.py:46
  1207.3 11.9 copy-start.8
  1207.3 11.9 copy-start.15
  1207.3 11.9 copy-start.18
  1207.4 11.9 copy-start.20
  1219.3 11.1 copy-start.29
  1219.3 37.9 %copy-start.5 = (f32[512,1536]{1,0:T(8,128)S(1)}, f32[512,1536]{1,0:T(8,128)}, u32[]{:S(2)}) copy-start(f32[512,1536]{1,0:T(8,128)} %copy-done.4) | copy-start | bytes 9437188
  (11 other events, 16.8 us)
Sparse Core Ops, SparseCore 0:
  9.9 61.4 all-gather.9
  85.2 115.3 all-gather.11
  202.5 36.9 all-gather.13
  241.2 125.1 all-gather.15
  368.2 72.0 all-gather.17
  560.7 252.2 reduce-scatter.5
  816.4 54.2 reduce-scatter.9
  874.2 92.2 reduce-scatter.13
  970.1 76.8 reduce-scatter.7
  1050.4 156.3 reduce-scatter.11
  1209.2 88.4 all-reduce.9
  1299.1 88.3 all-gather.19
  1389.1 216.5 all-gather.21
